TPU v7x, 32 devices: a whole 2x2x4 slice. The times are simulated.
32 devices in a mesh: groups: 2 (over x), row: 8 (over z, y), col: 2 (over core).
Axes of the slice: x: 2, y: 2, z: 4, core: 2. Of those that a mesh axis runs over, the one named last changes fastest.
Arguments:
- spectra: bfloat16 [4096, 16384], P(('groups', 'row', 'col')), parts along dimension 0, may hold values from -60 to 60
- block_order: int32 [4096], P('groups'), parts along dimension 0, may hold values from 0 to 2047, each once
- offsets: int32 [17], replicated, may hold values from -24 to 24, as said below
Outputs:
- similarity: float32 [4096, 2048], P(('groups', 'row', 'col')), parts along dimension 0
There are 2 independent parts, one for each index of `groups`. A program takes and returns all parts, laid end to end along the dimension named above; an argument that names none is the same for every part. Nothing has to cross between parts.
Inputs may be any that keep to these rules, and one draw needn't show every extreme that they name: `offsets`: the 17 values are distinct, include 0 and 24, and the negative of each value is also among them.
All inputs are finite; a program needn't handle non-finite values.
Results may differ from a plain program's by a relative error of at most 0.0013.
Values may be sent and summed in bfloat16 or wider, within the bound.
A program may use at most 128 MiB of HBM per device.

v0:
```python
import math
import jax
import jax.numpy as jnp
from jax import lax
from jax.sharding import PartitionSpec as P

TAPS = 16
PADW = 64


def taps_table(count):
    steps = jnp.arange(count, dtype=jnp.float32)
    return (0.5 - 0.5 * jnp.cos(2.0 * math.pi * (steps + 0.5) / count)).astype(jnp.bfloat16)


def shifted_stack(mine, offsets):
    coarse_len = mine.shape[1]
    mine_padded = jnp.pad(mine, ((0, 0), (PADW, PADW)))

    def moved(offset):
        return lax.dynamic_slice_in_dim(mine_padded, PADW - offset, coarse_len, 1)

    stacked = jax.vmap(moved)(offsets)
    return stacked.reshape(-1, coarse_len)


def strip_scores(stacked, extended, first_block, block_rows, width_blocks):
    panel = lax.dynamic_slice_in_dim(
        extended, first_block * block_rows, width_blocks * block_rows, 0
    )
    scores = lax.dot_general(
        stacked, panel, (((1,), (1,)), ((), ())), preferred_element_type=jnp.float32
    )
    scores = scores.reshape(-1, block_rows, width_blocks, block_rows)
    return jnp.max(scores, axis=0)


def per_device(spectra, block_order, offsets):
    block_rows, bins = spectra.shape
    coarse_len = bins // TAPS
    group = min(128, coarse_len)
    weights = jnp.kron(
        jnp.eye(group, dtype=jnp.float32), taps_table(TAPS).astype(jnp.float32)[:, None]
    ).astype(jnp.bfloat16)
    windows = spectra.reshape(block_rows * coarse_len // group, TAPS * group)
    coarse = jnp.dot(windows, weights, preferred_element_type=jnp.float32).reshape(
        block_rows, coarse_len
    )
    scale = lax.rsqrt(jnp.mean(coarse * coarse, axis=1, keepdims=True) + 1e-06) * (
        1.0 / math.sqrt(coarse_len)
    )
    unit = (coarse * scale).astype(jnp.bfloat16)
    every = lax.all_gather(unit, ("row", "col"), axis=0, tiled=True)
    ordered = jnp.take(every, block_order, axis=0)
    total_rows = ordered.shape[0]
    blocks = lax.axis_size("row") * lax.axis_size("col")
    myself = lax.axis_index("row") * lax.axis_size("col") + lax.axis_index("col")
    mine = lax.dynamic_slice_in_dim(ordered, myself * block_rows, block_rows, 0)
    stacked = shifted_stack(mine, offsets)
    extended = jnp.concatenate([ordered, ordered[:block_rows]], axis=0)
    empty = jnp.zeros((blocks, block_rows, block_rows), jnp.float32)

    def place(acc, first):
        scores = strip_scores(stacked, extended, first, block_rows, 2)
        acc = lax.dynamic_update_slice_in_dim(acc, scores[None, :, 0, :], first, 0)
        return lax.dynamic_update_slice_in_dim(acc, scores[None, :, 1, :], (first + 1) % blocks, 0)

    result = lax.fori_loop(0, blocks // 2, lambda pair, acc: place(acc, 2 * pair), empty)
    return jnp.transpose(result, (1, 0, 2)).reshape(block_rows, total_rows)


def solution(mesh):
    in_specs = (P(("groups", "row", "col"), None), P("groups"), P())
    out_specs = P(("groups", "row", "col"), None)
    return jax.shard_map(
        per_device, mesh=mesh, in_specs=in_specs, out_specs=out_specs, check_vma=False
    )
```

profile of v0, /device:TPU:0, one launch (start us, length us, event | category | flops | bytes accessed | tf_op | source)
XLA Modules:
  0.0 212.4 jit_solution(15265125319011555981)
XLA Ops:
  6.6 7.4 %reshape.96 = bf16[1024,2048]{1,0:T(8,128)(2,1)} reshape(bf16[128,16384]{1,0:T(8,128)(2,1)} %param.5) | data formatting | bytes 8388608 | tf_op jit(solution)/shard_map/reshape | solution.py:45
  14.2 3.7 %multiply_reduce_fusion = (f32[1024]{0:T(1024)S(1)}, f32[1024,128]{0,1:T(8,128)S(1)}) fusion(bf16[2048,128]{1,0:T(8,128)(2,1)S(1)} %bitcast.40, bf16[1024,2048]{1,0:T(8,128)(2,1)} %reshape.96), kind=kOutput, calls=%fused_computation.14 | convolution fusion | flops 537132032 | bytes 5246976 | tf_op jit(solution)/shard_map/dot_general | solution.py:46
  19.4 53.3 %all-gather.2.cloned.1.call-done = bf16[2048,1024]{1,0:T(8,128)(2,1)} async-done(((bf16[128,1024]{1,0:T(8,128)(2,1)}), bf16[2048,1024]{1,0:T(8,128)(2,1)}) %all-gather.2.cloned.1.call-update) | async-done | bytes 4194320 | tf_op jit(solution)/shard_map/all_gather | solution.py:53
  72.7 13.7 %gather_fusion = bf16[2048,1024]{1,0:T(8,128)(2,1)} fusion(bf16[2048,1024]{1,0:T(8,128)(2,1)} %all-gather.2.cloned.1.call-done, s32[2048]{0:T(1024)S(1)} %fusion.3), kind=kCustom, calls=%fused_computation | custom fusion | bytes 8396800 | tf_op jit(solution)/shard_map/jit(_take)/gather | solution.py:54
  86.4 2.5 %broadcast_select_fusion = bf16[2048,1024]{1,0:T(8,128)(2,1)S(1)} fusion(bf16[2048,1024]{1,0:T(8,128)(2,1)} %gather_fusion, pred[2048]{0:T(1024)(128)(4,1)S(1)} %compare_and_fusion), kind=kLoop, calls=%fused_computation.9 | loop fusion | flops 2097152 | bytes 8390656 | tf_op jit(solution)/shard_map/jit(_take)/select_n | solution.py:54
  89.0 2.5 %pad_maximum_fusion = bf16[2176,1024]{1,0:T(8,128)(2,1)} fusion(bf16[128,1024]{1,0:T(8,128)(2,1)S(1)} %get-tuple-element.145, bf16[2048,1024]{1,0:T(8,128)(2,1)S(1)} %broadcast_select_fusion), kind=kLoop, calls=%fused_computation.8 | loop fusion | flops 8912896 | bytes 8912896 | tf_op jit(solution)/shard_map/concatenate | solution.py:60
  91.7 35.6 %while.17 = (s32[]{:T(128)}, bf16[128,1152]{1,0:T(8,128)(2,1)S(1)}, s32[17,2]{0,1:T(2,128)S(1)}, bf16[17,128,1024]{2,1,0:T(8,128)(2,1)}, s32[]{:T(128)}) while((s32[]{:T(128)}, bf16[128,1152]{1,0:T(8,128)(2,1)S(1)}, s32[17,2]{0,1:T(2,128)S(1)}, bf16[17,128,1024]{2,1,0:T(8,128)(2,1)}, s32[]{:T(128)}) %tuple.52), condition=%wide.while_cond, body=%wide.while_body.sunk | while | flops 2 | bytes 525401 | solution.py:21
  92.3 1.5 bitcast_dynamic-update-slice_fusion.8
  94.3 1.5 bitcast_dynamic-update-slice_fusion.8
  96.4 1.5 bitcast_dynamic-update-slice_fusion.8
  98.5 1.5 bitcast_dynamic-update-slice_fusion.8
  100.6 1.5 bitcast_dynamic-update-slice_fusion.8
  102.7 1.5 bitcast_dynamic-update-slice_fusion.8
  104.8 1.5 bitcast_dynamic-update-slice_fusion.8
  106.9 1.5 bitcast_dynamic-update-slice_fusion.8
  109.0 1.5 bitcast_dynamic-update-slice_fusion.8
  111.1 1.5 bitcast_dynamic-update-slice_fusion.8
  113.2 1.5 bitcast_dynamic-update-slice_fusion.8
  117.4 1.5 bitcast_dynamic-update-slice_fusion.8
  119.4 1.5 bitcast_dynamic-update-slice_fusion.8
  121.5 1.5 bitcast_dynamic-update-slice_fusion.8
  123.6 1.5 bitcast_dynamic-update-slice_fusion.8
  125.7 1.5 bitcast_dynamic-update-slice_fusion.8
  127.3 77.2 %while.16 = (s32[]{:T(128)}, f32[16,128,128]{2,1,0:T(8,128)S(1)}, bf16[2176,1024]{1,0:T(8,128)(2,1)}, bf16[2176,1024]{1,0:T(8,128)(2,1)}, s32[]{:T(128)}, /*inde...) while((s32[]{:T(128)}, f32[16,128,128]{2,1,0:T(8,128)S(1)}, ...), condition=%wide.region_4.5_spmd, body=%wide.region_2.4_spmd.sunk | while | flops 1141374976 | bytes 19005812 | solution.py:68
  127.4 3.9 %convolution_bitcast_fusion.3 = f32[2176,256]{0,1:T(8,128)S(1)} fusion(bf16[2176,1024]{1,0:T(8,128)(2,1)} %get-tuple-element.244, bf16[2176,1024]{1,0:T(8,128)(2,1)} %get-tuple-element.243, s32[]{:T(128)S(6)} %select_n.83), kind=kOutput, calls=%fused_computation.1.clone.1 | convolution fusion | flops 1140850688 | bytes 7208964 | tf_op jit(solution)/shard_map/while/body/eval_jaxpr/dot_general | solution.py:31
  131.2 2.0 copy.14
  133.2 2.7 %reshape.129 = f32[17,128,2,128]{3,2,1,0:T(2,128)S(1)} reshape(f32[2176,256]{1,0:T(8,128)} %copy.14) | data formatting | bytes 4456448 | tf_op jit(solution)/shard_map/while/body/eval_jaxpr/reshape | solution.py:34
  137.0 3.9 %convolution_bitcast_fusion.3 = f32[2176,256]{0,1:T(8,128)S(1)} fusion(bf16[2176,1024]{1,0:T(8,128)(2,1)} %get-tuple-element.244, bf16[2176,1024]{1,0:T(8,128)(2,1)} %get-tuple-element.243, s32[]{:T(128)S(6)} %select_n.83), kind=kOutput, calls=%fused_computation.1.clone.1 | convolution fusion | flops 1140850688 | bytes 7208964 | tf_op jit(solution)/shard_map/while/body/eval_jaxpr/dot_general | solution.py:31
  140.9 2.0 copy.14
  142.8 2.7 %reshape.129 = f32[17,128,2,128]{3,2,1,0:T(2,128)S(1)} reshape(f32[2176,256]{1,0:T(8,128)} %copy.14) | data formatting | bytes 4456448 | tf_op jit(solution)/shard_map/while/body/eval_jaxpr/reshape | solution.py:34
  146.7 3.9 %convolution_bitcast_fusion.3 = f32[2176,256]{0,1:T(8,128)S(1)} fusion(bf16[2176,1024]{1,0:T(8,128)(2,1)} %get-tuple-element.244, bf16[2176,1024]{1,0:T(8,128)(2,1)} %get-tuple-element.243, s32[]{:T(128)S(6)} %select_n.83), kind=kOutput, calls=%fused_computation.1.clone.1 | convolution fusion | flops 1140850688 | bytes 7208964 | tf_op jit(solution)/shard_map/while/body/eval_jaxpr/dot_general | solution.py:31
  150.5 2.0 copy.14
  152.5 2.7 %reshape.129 = f32[17,128,2,128]{3,2,1,0:T(2,128)S(1)} reshape(f32[2176,256]{1,0:T(8,128)} %copy.14) | data formatting | bytes 4456448 | tf_op jit(solution)/shard_map/while/body/eval_jaxpr/reshape | solution.py:34
  156.3 3.9 %convolution_bitcast_fusion.3 = f32[2176,256]{0,1:T(8,128)S(1)} fusion(bf16[2176,1024]{1,0:T(8,128)(2,1)} %get-tuple-element.244, bf16[2176,1024]{1,0:T(8,128)(2,1)} %get-tuple-element.243, s32[]{:T(128)S(6)} %select_n.83), kind=kOutput, calls=%fused_computation.1.clone.1 | convolution fusion | flops 1140850688 | bytes 7208964 | tf_op jit(solution)/shard_map/while/body/eval_jaxpr/dot_general | solution.py:31
  160.2 2.0 copy.14
  162.1 2.7 %reshape.129 = f32[17,128,2,128]{3,2,1,0:T(2,128)S(1)} reshape(f32[2176,256]{1,0:T(8,128)} %copy.14) | data formatting | bytes 4456448 | tf_op jit(solution)/shard_map/while/body/eval_jaxpr/reshape | solution.py:34
  165.9 3.9 %convolution_bitcast_fusion.3 = f32[2176,256]{0,1:T(8,128)S(1)} fusion(bf16[2176,1024]{1,0:T(8,128)(2,1)} %get-tuple-element.244, bf16[2176,1024]{1,0:T(8,128)(2,1)} %get-tuple-element.243, s32[]{:T(128)S(6)} %select_n.83), kind=kOutput, calls=%fused_computation.1.clone.1 | convolution fusion | flops 1140850688 | bytes 7208964 | tf_op jit(solution)/shard_map/while/body/eval_jaxpr/dot_general | solution.py:31
  169.8 2.0 copy.14
  171.8 2.7 %reshape.129 = f32[17,128,2,128]{3,2,1,0:T(2,128)S(1)} reshape(f32[2176,256]{1,0:T(8,128)} %copy.14) | data formatting | bytes 4456448 | tf_op jit(solution)/shard_map/while/body/eval_jaxpr/reshape | solution.py:34
  175.6 3.9 %convolution_bitcast_fusion.3 = f32[2176,256]{0,1:T(8,128)S(1)} fusion(bf16[2176,1024]{1,0:T(8,128)(2,1)} %get-tuple-element.244, bf16[2176,1024]{1,0:T(8,128)(2,1)} %get-tuple-element.243, s32[]{:T(128)S(6)} %select_n.83), kind=kOutput, calls=%fused_computation.1.clone.1 | convolution fusion | flops 1140850688 | bytes 7208964 | tf_op jit(solution)/shard_map/while/body/eval_jaxpr/dot_general | solution.py:31
  179.5 2.0 copy.14
  181.4 2.7 %reshape.129 = f32[17,128,2,128]{3,2,1,0:T(2,128)S(1)} reshape(f32[2176,256]{1,0:T(8,128)} %copy.14) | data formatting | bytes 4456448 | tf_op jit(solution)/shard_map/while/body/eval_jaxpr/reshape | solution.py:34
  185.2 3.9 %convolution_bitcast_fusion.3 = f32[2176,256]{0,1:T(8,128)S(1)} fusion(bf16[2176,1024]{1,0:T(8,128)(2,1)} %get-tuple-element.244, bf16[2176,1024]{1,0:T(8,128)(2,1)} %get-tuple-element.243, s32[]{:T(128)S(6)} %select_n.83), kind=kOutput, calls=%fused_computation.1.clone.1 | convolution fusion | flops 1140850688 | bytes 7208964 | tf_op jit(solution)/shard_map/while/body/eval_jaxpr/dot_general | solution.py:31
  189.1 2.0 copy.14
  191.1 2.7 %reshape.129 = f32[17,128,2,128]{3,2,1,0:T(2,128)S(1)} reshape(f32[2176,256]{1,0:T(8,128)} %copy.14) | data formatting | bytes 4456448 | tf_op jit(solution)/shard_map/while/body/eval_jaxpr/reshape | solution.py:34
  194.9 3.9 %convolution_bitcast_fusion.3 = f32[2176,256]{0,1:T(8,128)S(1)} fusion(bf16[2176,1024]{1,0:T(8,128)(2,1)} %get-tuple-element.244, bf16[2176,1024]{1,0:T(8,128)(2,1)} %get-tuple-element.243, s32[]{:T(128)S(6)} %select_n.83), kind=kOutput, calls=%fused_computation.1.clone.1 | convolution fusion | flops 1140850688 | bytes 7208964 | tf_op jit(solution)/shard_map/while/body/eval_jaxpr/dot_general | solution.py:31
  198.8 2.0 copy.14
  200.7 2.7 %reshape.129 = f32[17,128,2,128]{3,2,1,0:T(2,128)S(1)} reshape(f32[2176,256]{1,0:T(8,128)} %copy.14) | data formatting | bytes 4456448 | tf_op jit(solution)/shard_map/while/body/eval_jaxpr/reshape | solution.py:34
  (91 shorter events, 22.2 us)
Async XLA Ops:
  6.5 66.1 %all-gather.2.cloned.1.call-start = ((), (), s32[]{:S(2)}) async-start(), calls=%async_computation | async-start | bytes 4456448 | tf_op jit(solution)/shard_map/all_gather | solution.py:53
  14.2 5.1 %copy-start.1 = (s32[17]{0:T(128)S(1)}, s32[17]{0:T(128)}, u32[]{:S(2)}) copy-start(s32[17]{0:T(128)} %param.7) | copy-start | bytes 208
  14.2 5.2 %copy-start = (s32[2048]{0:T(1024)S(1)}, s32[2048]{0:T(1024)}, u32[]{:S(2)}) copy-start(s32[2048]{0:T(1024)} %param.6) | copy-start | bytes 24580
Sparse Core Ops, SparseCore 0:
  19.4 53.2 all-gather.1
where the time goes:
time: 213 us; the launch traced here: 212 us
  local copies, waits for them, and re-layouts  97.1 us (46%)
  waiting for transfers between devices  53.3 us (25%)
  matrix products  34.6 us (16%)
  between operations  13.6 us (6%)
  other arithmetic  13 us (6%)
    all_gather x1, waiting for transfers between devices, per_device(): every = lax.all_gather(unit, ('row', 'col'), axis=0, tiled=True)  53.3 us
    gather x51, local copies, waits for them, and re-layouts  35.5 us
    dot_general x8, matrix products, strip_scores(): lax.dot_general(stacked, panel, (((1,), (1,)), ((), ())), preferred_eleme...  30.8 us
    reshape x8, local copies, waits for them, and re-layouts, strip_scores(): scores = scores.reshape(-1, block_rows, width_blocks, block_rows)  22 us
    dot_general x8, local copies, waits for them, and re-layouts, strip_scores(): lax.dot_general(stacked, panel, (((1,), (1,)), ((), ())), preferred_eleme...  15.8 us
    gather x1, local copies, waits for them, and re-layouts, per_device(): ordered = jnp.take(every, block_order, axis=0)  13.7 us
    reshape x1, local copies, waits for them, and re-layouts, per_device(): windows = spectra.reshape(block_rows * coarse_len // group, TAPS * group)  7.39 us
    reduce_max x8, other arithmetic, strip_scores(): return jnp.max(scores, axis=0)  6.83 us
  transfers between devices with their start and end apart: 1, of which 1 were waited for; matrix products, arithmetic and copies ran while one was open for 0% of the time, Pallas kernels for 0%

commit v1 on v0

--- a/solution.py
+++ b/solution.py
@@ -6,6 +6,22 @@
 
 TAPS = 16
 PADW = 64
+
+
+def collect(x, axis, dim):
+    ways, here, hop = (lax.axis_size(axis), lax.axis_index(axis), x.shape[dim])
+    dims = [n * ways if d == dim else n for d, n in enumerate(x.shape)]
+    full = lax.dynamic_update_slice_in_dim(jnp.zeros(dims, x.dtype), x, here * hop, axis=dim)
+    going_up = going_down = x
+    for far in range(1, ways // 2 + 1):
+        going_up = lax.ppermute(going_up, axis, [(d, (d + 1) % ways) for d in range(ways)])
+        full = lax.dynamic_update_slice_in_dim(full, going_up, (here - far) % ways * hop, axis=dim)
+        if 2 * far < ways:
+            going_down = lax.ppermute(going_down, axis, [(d, (d - 1) % ways) for d in range(ways)])
+            full = lax.dynamic_update_slice_in_dim(
+                full, going_down, (here + far) % ways * hop, axis=dim
+            )
+    return full
 
 
 def taps_table(count):
@@ -50,7 +66,7 @@
         1.0 / math.sqrt(coarse_len)
     )
     unit = (coarse * scale).astype(jnp.bfloat16)
-    every = lax.all_gather(unit, ("row", "col"), axis=0, tiled=True)
+    every = collect(unit, ("row", "col"), 0)
     ordered = jnp.take(every, block_order, axis=0)
     total_rows = ordered.shape[0]
     blocks = lax.axis_size("row") * lax.axis_size("col")

time: 213 us -> 222 us (1.042)
  starting transfers between devices: 0.01 us -> 32 us
  waiting for transfers between devices: 53.3 us -> 27.2 us
  between operations: 13.6 us -> 0.51 us
  local copies, waits for them, and re-layouts: 97.1 us -> 110 us
  other arithmetic: 13 us -> 15.3 us
    all_gather x1 -> x0, waiting for transfers between devices: 53.3 us -> none  [per_device(): every = lax.all_gather(unit, ('row', 'col'), axis=0, tiled=True)]
    ppermute x0 -> x15, starting transfers between devices: none -> 32 us  [the longest x7 31.5 us: collect(): lax.ppermute(going_down, axis, [(d, (d - 1) % ways) for d in range(ways)])]
    ppermute x0 -> x15, waiting for transfers between devices: none -> 27.2 us  [the longest x8 27.1 us: collect(): lax.ppermute(going_up, axis, [(d, (d + 1) % ways) for d in range(ways)])]
    dynamic_update_slice x0 -> x15, local copies, waits for them, and re-layouts: none -> 10.9 us  [the longest x8 5.78 us: collect(): lax.dynamic_update_slice_in_dim(full, going_up, (here - far) % ways * hop...]
    broadcast_in_dim x0 -> x1, local copies, waits for them, and re-layouts: none -> 2.56 us  [collect(): jnp.zeros(dims, x.dtype)]
    concatenate x1, other arithmetic: 2.52 us -> 4.77 us  [per_device(): extended = jnp.concatenate([ordered, ordered[:block_rows]], axis=0)]
    gather x51, local copies, waits for them, and re-layouts: 35.5 us -> 33.3 us
  transfers between devices with their start and end apart: 1 -> 15, of which waited for: 1 -> 8; matrix products, arithmetic and copies ran while one was open for 0% -> 5% of each run, Pallas kernels for 0% -> 0%
where the time goes in v1:
time: 222 us; the launch traced here: 221 us
  local copies, waits for them, and re-layouts  110 us (50%)
  matrix products  34.6 us (16%)
  starting transfers between devices  32 us (14%)
  waiting for transfers between devices  27.2 us (12%)
  other arithmetic  15.3 us (7%)
    gather x51, local copies, waits for them, and re-layouts  33.3 us
    ppermute x7, starting transfers between devices, collect(): lax.ppermute(going_down, axis, [(d, (d - 1) % ways) for d in range(ways)])  31.5 us
    dot_general x8, matrix products, strip_scores(): lax.dot_general(stacked, panel, (((1,), (1,)), ((), ())), preferred_eleme...  30.8 us
    ppermute x8, waiting for transfers between devices, collect(): lax.ppermute(going_up, axis, [(d, (d + 1) % ways) for d in range(ways)])  27.1 us
    reshape x8, local copies, waits for them, and re-layouts, strip_scores(): scores = scores.reshape(-1, block_rows, width_blocks, block_rows)  22 us
    dot_general x8, local copies, waits for them, and re-layouts, strip_scores(): lax.dot_general(stacked, panel, (((1,), (1,)), ((), ())), preferred_eleme...  15.7 us
    gather x1, local copies, waits for them, and re-layouts, per_device(): ordered = jnp.take(every, block_order, axis=0)  13.7 us
    reshape x1, local copies, waits for them, and re-layouts, per_device(): windows = spectra.reshape(block_rows * coarse_len // group, TAPS * group)  7.41 us
  transfers between devices with their start and end apart: 15, of which 8 were waited for; matrix products, arithmetic and copies ran while one was open for 5% of the time, Pallas kernels for 0%

profile of v1, /device:TPU:0, one launch (start us, length us, event | category | flops | bytes accessed | tf_op | source)
XLA Modules:
  0.0 220.7 jit_solution(7567981317895701346)
XLA Ops:
  0.1 7.4 %reshape.96 = bf16[1024,2048]{1,0:T(8,128)(2,1)} reshape(bf16[128,16384]{1,0:T(8,128)(2,1)} %param.5) | data formatting | bytes 8388608 | tf_op jit(solution)/shard_map/reshape | solution.py:61
  7.6 3.7 %multiply_reduce_fusion = (f32[1024]{0:T(1024)S(1)}, f32[1024,128]{0,1:T(8,128)S(1)}) fusion(bf16[2048,128]{1,0:T(8,128)(2,1)S(1)} %bitcast.40, bf16[1024,2048]{1,0:T(8,128)(2,1)} %reshape.96), kind=kOutput, calls=%fused_computation.14 | convolution fusion | flops 537132032 | bytes 5246976 | tf_op jit(solution)/shard_map/dot_general | solution.py:62
  11.9 2.6 %broadcast_in_dim.29 = bf16[2048,1024]{1,0:T(8,128)(2,1)} broadcast(bf16[]{:T(256)} %constant.207.clone.1), dimensions={} | broadcast | bytes 4194306 | tf_op jit(solution)/shard_map/broadcast_in_dim | solution.py:14
  15.8 5.0 %collective-permute-start.1 = (bf16[128,1024]{1,0:T(8,128)(2,1)S(1)}, bf16[128,1024]{1,0:T(8,128)(2,1)S(1)}, u32[]{:S(2)}, u32[]{:S(2)}) collective-permute-start(bf16[128,1024]{1,0:T(8,128)(2,1)S(1)} %get-tuple-element.143), channel_id=1, source_target_pairs={{0,15},{1,0},{2,1},{3,2},{4,3},{5,4},{6,5},{7,6},{8,7},{9,8},{10,9... | collective-permute-start | bytes 786440 | tf_op jit(solution)/shard_map/ppermute | solution.py:20
  20.7 4.2 %collective-permute-done = bf16[128,1024]{1,0:T(8,128)(2,1)S(1)} collective-permute-done((bf16[128,1024]{1,0:T(8,128)(2,1)S(1)}, bf16[128,1024]{1,0:T(8,128)(2,1)S(1)}, u32[]{:S(2)}, u32[]{:S(2)}) %collective-permute-start) | collective-permute-done | bytes 262176 | tf_op jit(solution)/shard_map/ppermute | solution.py:17
  24.9 4.4 %collective-permute-start.3 = (bf16[128,1024]{1,0:T(8,128)(2,1)S(1)}, bf16[128,1024]{1,0:T(8,128)(2,1)S(1)}, u32[]{:S(2)}, u32[]{:S(2)}) collective-permute-start(bf16[128,1024]{1,0:T(8,128)(2,1)S(1)} %collective-permute-done.1), channel_id=1, source_target_pairs={{0,15},{1,0},{2,1},{3,2},{4,3},{5,4},{6,5},{7,6},{8,7},{9,8},{10,9... | collective-permute-start | bytes 786440 | tf_op jit(solution)/shard_map/ppermute | solution.py:20
  29.3 4.2 %collective-permute-done.2 = bf16[128,1024]{1,0:T(8,128)(2,1)S(1)} collective-permute-done((bf16[128,1024]{1,0:T(8,128)(2,1)S(1)}, bf16[128,1024]{1,0:T(8,128)(2,1)S(1)}, u32[]{:S(2)}, u32[]{:S(2)}) %collective-permute-start.2) | collective-permute-done | bytes 262176 | tf_op jit(solution)/shard_map/ppermute | solution.py:17
  33.5 4.5 %collective-permute-start.5 = (bf16[128,1024]{1,0:T(8,128)(2,1)S(1)}, bf16[128,1024]{1,0:T(8,128)(2,1)S(1)}, u32[]{:S(2)}, u32[]{:S(2)}) collective-permute-start(bf16[128,1024]{1,0:T(8,128)(2,1)S(1)} %collective-permute-done.3), channel_id=1, source_target_pairs={{0,15},{1,0},{2,1},{3,2},{4,3},{5,4},{6,5},{7,6},{8,7},{9,8},{10,9... | collective-permute-start | bytes 786440 | tf_op jit(solution)/shard_map/ppermute | solution.py:20
  38.0 4.1 %collective-permute-done.4 = bf16[128,1024]{1,0:T(8,128)(2,1)S(1)} collective-permute-done((bf16[128,1024]{1,0:T(8,128)(2,1)S(1)}, bf16[128,1024]{1,0:T(8,128)(2,1)S(1)}, u32[]{:S(2)}, u32[]{:S(2)}) %collective-permute-start.4) | collective-permute-done | bytes 262176 | tf_op jit(solution)/shard_map/ppermute | solution.py:17
  43.2 4.2 %collective-permute-start.7 = (bf16[128,1024]{1,0:T(8,128)(2,1)S(1)}, bf16[128,1024]{1,0:T(8,128)(2,1)S(1)}, u32[]{:S(2)}, u32[]{:S(2)}) collective-permute-start(bf16[128,1024]{1,0:T(8,128)(2,1)S(1)} %collective-permute-done.5), channel_id=1, source_target_pairs={{0,15},{1,0},{2,1},{3,2},{4,3},{5,4},{6,5},{7,6},{8,7},{9,8},{10,9... | collective-permute-start | bytes 786440 | tf_op jit(solution)/shard_map/ppermute | solution.py:20
  48.1 2.6 %collective-permute-done.6 = bf16[128,1024]{1,0:T(8,128)(2,1)S(1)} collective-permute-done((bf16[128,1024]{1,0:T(8,128)(2,1)S(1)}, bf16[128,1024]{1,0:T(8,128)(2,1)S(1)}, u32[]{:S(2)}, u32[]{:S(2)}) %collective-permute-start.6) | collective-permute-done | bytes 262176 | tf_op jit(solution)/shard_map/ppermute | solution.py:17
  52.1 4.5 %collective-permute-start.9 = (bf16[128,1024]{1,0:T(8,128)(2,1)S(1)}, bf16[128,1024]{1,0:T(8,128)(2,1)S(1)}, u32[]{:S(2)}, u32[]{:S(2)}) collective-permute-start(bf16[128,1024]{1,0:T(8,128)(2,1)S(1)} %collective-permute-done.7), channel_id=1, source_target_pairs={{0,15},{1,0},{2,1},{3,2},{4,3},{5,4},{6,5},{7,6},{8,7},{9,8},{10,9... | collective-permute-start | bytes 786440 | tf_op jit(solution)/shard_map/ppermute | solution.py:20
  57.3 1.9 collective-permute-done.8
  60.8 4.5 %collective-permute-start.11 = (bf16[128,1024]{1,0:T(8,128)(2,1)S(1)}, bf16[128,1024]{1,0:T(8,128)(2,1)S(1)}, u32[]{:S(2)}, u32[]{:S(2)}) collective-permute-start(bf16[128,1024]{1,0:T(8,128)(2,1)S(1)} %collective-permute-done.9), channel_id=1, source_target_pairs={{0,15},{1,0},{2,1},{3,2},{4,3},{5,4},{6,5},{7,6},{8,7},{9,8},{10,9... | collective-permute-start | bytes 786440 | tf_op jit(solution)/shard_map/ppermute | solution.py:20
  65.9 2.0 collective-permute-done.10
  69.3 4.5 %collective-permute-start.13 = (bf16[128,1024]{1,0:T(8,128)(2,1)S(1)}, bf16[128,1024]{1,0:T(8,128)(2,1)S(1)}, u32[]{:S(2)}, u32[]{:S(2)}) collective-permute-start(bf16[128,1024]{1,0:T(8,128)(2,1)S(1)} %collective-permute-done.11), channel_id=1, source_target_pairs={{0,15},{1,0},{2,1},{3,2},{4,3},{5,4},{6,5},{7,6},{8,7},{9,8},{10,9... | collective-permute-start | bytes 786440 | tf_op jit(solution)/shard_map/ppermute | solution.py:20
  74.5 2.0 collective-permute-done.12
  78.7 6.3 %collective-permute-done.14 = bf16[128,1024]{1,0:T(8,128)(2,1)S(1)} collective-permute-done((bf16[128,1024]{1,0:T(8,128)(2,1)S(1)}, bf16[128,1024]{1,0:T(8,128)(2,1)S(1)}, u32[]{:S(2)}, u32[]{:S(2)}) %collective-permute-start.14) | collective-permute-done | bytes 262176 | tf_op jit(solution)/shard_map/ppermute | solution.py:17
  85.7 13.7 %gather_fusion = bf16[2048,1024]{1,0:T(8,128)(2,1)} fusion(bf16[2048,1024]{1,0:T(8,128)(2,1)} %constant_dynamic-update-slice_fusion, s32[2048]{0:T(1024)S(1)} %fusion.3), kind=kCustom, calls=%fused_computation | custom fusion | bytes 8396800 | tf_op jit(solution)/shard_map/jit(_take)/gather | solution.py:70
  99.5 2.5 %broadcast_select_fusion = bf16[2048,1024]{1,0:T(8,128)(2,1)S(1)} fusion(bf16[2048,1024]{1,0:T(8,128)(2,1)} %gather_fusion, pred[2048]{0:T(1024)(128)(4,1)S(1)} %compare_and_fusion), kind=kLoop, calls=%fused_computation.9 | loop fusion | flops 2097152 | bytes 8390656 | tf_op jit(solution)/shard_map/jit(_take)/select_n | solution.py:70
  102.0 2.0 copy-done
  104.2 33.3 %while.17 = (s32[]{:T(128)}, bf16[128,1152]{1,0:T(8,128)(2,1)S(1)}, s32[17,2]{0,1:T(2,128)S(1)}, bf16[17,128,1024]{2,1,0:T(8,128)(2,1)}, s32[]{:T(128)}) while((s32[]{:T(128)}, bf16[128,1152]{1,0:T(8,128)(2,1)S(1)}, s32[17,2]{0,1:T(2,128)S(1)}, bf16[17,128,1024]{2,1,0:T(8,128)(2,1)}, s32[]{:T(128)}) %tuple.53), condition=%wide.while_cond, body=%wide.while_body.sunk | while | flops 2 | bytes 525401 | solution.py:37
  137.5 4.8 %pad_maximum_fusion = bf16[2176,1024]{1,0:T(8,128)(2,1)} fusion(bf16[128,1024]{1,0:T(8,128)(2,1)S(1)} %get-tuple-element.147, bf16[2048,1024]{1,0:T(8,128)(2,1)} %copy-done), kind=kLoop, calls=%fused_computation.8 | loop fusion | flops 8912896 | bytes 8912896 | tf_op jit(solution)/shard_map/concatenate | solution.py:76
  142.4 77.2 %while.16 = (s32[]{:T(128)}, f32[16,128,128]{2,1,0:T(8,128)S(1)}, bf16[2176,1024]{1,0:T(8,128)(2,1)}, bf16[2176,1024]{1,0:T(8,128)(2,1)}, s32[]{:T(128)}, /*inde...) while((s32[]{:T(128)}, f32[16,128,128]{2,1,0:T(8,128)S(1)}, ...), condition=%wide.region_4.5_spmd, body=%wide.region_2.4_spmd.sunk | while | flops 1141374976 | bytes 19005812 | solution.py:84
  142.4 3.9 %convolution_bitcast_fusion.3 = f32[2176,256]{0,1:T(8,128)S(1)} fusion(bf16[2176,1024]{1,0:T(8,128)(2,1)} %get-tuple-element.246, bf16[2176,1024]{1,0:T(8,128)(2,1)} %get-tuple-element.245, s32[]{:T(128)S(6)} %select_n.222), kind=kOutput, calls=%fused_computation.1.clone.1 | convolution fusion | flops 1140850688 | bytes 7208964 | tf_op jit(solution)/shard_map/while/body/eval_jaxpr/dot_general | solution.py:47
  146.3 2.0 copy.14
  148.3 2.7 %reshape.129 = f32[17,128,2,128]{3,2,1,0:T(2,128)S(1)} reshape(f32[2176,256]{1,0:T(8,128)} %copy.14) | data formatting | bytes 4456448 | tf_op jit(solution)/shard_map/while/body/eval_jaxpr/reshape | solution.py:50
  152.1 3.9 %convolution_bitcast_fusion.3 = f32[2176,256]{0,1:T(8,128)S(1)} fusion(bf16[2176,1024]{1,0:T(8,128)(2,1)} %get-tuple-element.246, bf16[2176,1024]{1,0:T(8,128)(2,1)} %get-tuple-element.245, s32[]{:T(128)S(6)} %select_n.222), kind=kOutput, calls=%fused_computation.1.clone.1 | convolution fusion | flops 1140850688 | bytes 7208964 | tf_op jit(solution)/shard_map/while/body/eval_jaxpr/dot_general | solution.py:47
  155.9 2.0 copy.14
  157.9 2.7 %reshape.129 = f32[17,128,2,128]{3,2,1,0:T(2,128)S(1)} reshape(f32[2176,256]{1,0:T(8,128)} %copy.14) | data formatting | bytes 4456448 | tf_op jit(solution)/shard_map/while/body/eval_jaxpr/reshape | solution.py:50
  161.7 3.9 %convolution_bitcast_fusion.3 = f32[2176,256]{0,1:T(8,128)S(1)} fusion(bf16[2176,1024]{1,0:T(8,128)(2,1)} %get-tuple-element.246, bf16[2176,1024]{1,0:T(8,128)(2,1)} %get-tuple-element.245, s32[]{:T(128)S(6)} %select_n.222), kind=kOutput, calls=%fused_computation.1.clone.1 | convolution fusion | flops 1140850688 | bytes 7208964 | tf_op jit(solution)/shard_map/while/body/eval_jaxpr/dot_general | solution.py:47
  165.6 2.0 copy.14
  167.6 2.7 %reshape.129 = f32[17,128,2,128]{3,2,1,0:T(2,128)S(1)} reshape(f32[2176,256]{1,0:T(8,128)} %copy.14) | data formatting | bytes 4456448 | tf_op jit(solution)/shard_map/while/body/eval_jaxpr/reshape | solution.py:50
  171.4 3.9 %convolution_bitcast_fusion.3 = f32[2176,256]{0,1:T(8,128)S(1)} fusion(bf16[2176,1024]{1,0:T(8,128)(2,1)} %get-tuple-element.246, bf16[2176,1024]{1,0:T(8,128)(2,1)} %get-tuple-element.245, s32[]{:T(128)S(6)} %select_n.222), kind=kOutput, calls=%fused_computation.1.clone.1 | convolution fusion | flops 1140850688 | bytes 7208964 | tf_op jit(solution)/shard_map/while/body/eval_jaxpr/dot_general | solution.py:47
  175.2 2.0 copy.14
  177.2 2.7 %reshape.129 = f32[17,128,2,128]{3,2,1,0:T(2,128)S(1)} reshape(f32[2176,256]{1,0:T(8,128)} %copy.14) | data formatting | bytes 4456448 | tf_op jit(solution)/shard_map/while/body/eval_jaxpr/reshape | solution.py:50
  181.0 3.9 %convolution_bitcast_fusion.3 = f32[2176,256]{0,1:T(8,128)S(1)} fusion(bf16[2176,1024]{1,0:T(8,128)(2,1)} %get-tuple-element.246, bf16[2176,1024]{1,0:T(8,128)(2,1)} %get-tuple-element.245, s32[]{:T(128)S(6)} %select_n.222), kind=kOutput, calls=%fused_computation.1.clone.1 | convolution fusion | flops 1140850688 | bytes 7208964 | tf_op jit(solution)/shard_map/while/body/eval_jaxpr/dot_general | solution.py:47
  184.9 2.0 copy.14
  186.9 2.7 %reshape.129 = f32[17,128,2,128]{3,2,1,0:T(2,128)S(1)} reshape(f32[2176,256]{1,0:T(8,128)} %copy.14) | data formatting | bytes 4456448 | tf_op jit(solution)/shard_map/while/body/eval_jaxpr/reshape | solution.py:50
  190.7 3.9 %convolution_bitcast_fusion.3 = f32[2176,256]{0,1:T(8,128)S(1)} fusion(bf16[2176,1024]{1,0:T(8,128)(2,1)} %get-tuple-element.246, bf16[2176,1024]{1,0:T(8,128)(2,1)} %get-tuple-element.245, s32[]{:T(128)S(6)} %select_n.222), kind=kOutput, calls=%fused_computation.1.clone.1 | convolution fusion | flops 1140850688 | bytes 7208964 | tf_op jit(solution)/shard_map/while/body/eval_jaxpr/dot_general | solution.py:47
  194.5 2.0 copy.14
  196.5 2.7 %reshape.129 = f32[17,128,2,128]{3,2,1,0:T(2,128)S(1)} reshape(f32[2176,256]{1,0:T(8,128)} %copy.14) | data formatting | bytes 4456448 | tf_op jit(solution)/shard_map/while/body/eval_jaxpr/reshape | solution.py:50
  200.3 3.9 %convolution_bitcast_fusion.3 = f32[2176,256]{0,1:T(8,128)S(1)} fusion(bf16[2176,1024]{1,0:T(8,128)(2,1)} %get-tuple-element.246, bf16[2176,1024]{1,0:T(8,128)(2,1)} %get-tuple-element.245, s32[]{:T(128)S(6)} %select_n.222), kind=kOutput, calls=%fused_computation.1.clone.1 | convolution fusion | flops 1140850688 | bytes 7208964 | tf_op jit(solution)/shard_map/while/body/eval_jaxpr/dot_general | solution.py:47
  204.2 2.0 copy.14
  206.2 2.7 %reshape.129 = f32[17,128,2,128]{3,2,1,0:T(2,128)S(1)} reshape(f32[2176,256]{1,0:T(8,128)} %copy.14) | data formatting | bytes 4456448 | tf_op jit(solution)/shard_map/while/body/eval_jaxpr/reshape | solution.py:50
  210.0 3.9 %convolution_bitcast_fusion.3 = f32[2176,256]{0,1:T(8,128)S(1)} fusion(bf16[2176,1024]{1,0:T(8,128)(2,1)} %get-tuple-element.246, bf16[2176,1024]{1,0:T(8,128)(2,1)} %get-tuple-element.245, s32[]{:T(128)S(6)} %select_n.222), kind=kOutput, calls=%fused_computation.1.clone.1 | convolution fusion | flops 1140850688 | bytes 7208964 | tf_op jit(solution)/shard_map/while/body/eval_jaxpr/dot_general | solution.py:47
  213.8 2.0 copy.14
  215.8 2.7 %reshape.129 = f32[17,128,2,128]{3,2,1,0:T(2,128)S(1)} reshape(f32[2176,256]{1,0:T(8,128)} %copy.14) | data formatting | bytes 4456448 | tf_op jit(solution)/shard_map/while/body/eval_jaxpr/reshape | solution.py:50
  (136 shorter events, 55.4 us)
Async XLA Ops:
  11.4 22.1 %copy-start.1 = (s32[2048]{0:T(1024)S(1)}, s32[2048]{0:T(1024)}, u32[]{:S(2)}) copy-start(s32[2048]{0:T(1024)} %param.6) | copy-start | bytes 24580
  11.4 30.7 %copy-start.2 = (s32[17]{0:T(128)S(1)}, s32[17]{0:T(128)}, u32[]{:S(2)}) copy-start(s32[17]{0:T(128)} %param.7) | copy-start | bytes 208
  15.3 9.6 %collective-permute-start = (bf16[128,1024]{1,0:T(8,128)(2,1)S(1)}, bf16[128,1024]{1,0:T(8,128)(2,1)S(1)}, u32[]{:S(2)}, u32[]{:S(2)}) collective-permute-start(bf16[128,1024]{1,0:T(8,128)(2,1)S(1)} %get-tuple-element.143), channel_id=1, source_target_pairs={{0,1},{1,2},{2,3},{3,4},{4,5},{5,6},{6,7},{7,8},{8,9},{9,10},{10,1... | collective-permute-start | bytes 786440 | tf_op jit(solution)/shard_map/ppermute | solution.py:17
  15.8 9.1 %collective-permute-start.1 = (bf16[128,1024]{1,0:T(8,128)(2,1)S(1)}, bf16[128,1024]{1,0:T(8,128)(2,1)S(1)}, u32[]{:S(2)}, u32[]{:S(2)}) collective-permute-start(bf16[128,1024]{1,0:T(8,128)(2,1)S(1)} %get-tuple-element.143), channel_id=1, source_target_pairs={{0,15},{1,0},{2,1},{3,2},{4,3},{5,4},{6,5},{7,6},{8,7},{9,8},{10,9... | collective-permute-start | bytes 786440 | tf_op jit(solution)/shard_map/ppermute | solution.py:20
  24.9 8.6 %collective-permute-start.2 = (bf16[128,1024]{1,0:T(8,128)(2,1)S(1)}, bf16[128,1024]{1,0:T(8,128)(2,1)S(1)}, u32[]{:S(2)}, u32[]{:S(2)}) collective-permute-start(bf16[128,1024]{1,0:T(8,128)(2,1)S(1)} %collective-permute-done), channel_id=1, source_target_pairs={{0,1},{1,2},{2,3},{3,4},{4,5},{5,6},{6,7},{7,8},{8,9},{9,10},{10,1... | collective-permute-start | bytes 786440 | tf_op jit(solution)/shard_map/ppermute | solution.py:17
  24.9 8.6 %collective-permute-start.3 = (bf16[128,1024]{1,0:T(8,128)(2,1)S(1)}, bf16[128,1024]{1,0:T(8,128)(2,1)S(1)}, u32[]{:S(2)}, u32[]{:S(2)}) collective-permute-start(bf16[128,1024]{1,0:T(8,128)(2,1)S(1)} %collective-permute-done.1), channel_id=1, source_target_pairs={{0,15},{1,0},{2,1},{3,2},{4,3},{5,4},{6,5},{7,6},{8,7},{9,8},{10,9... | collective-permute-start | bytes 786440 | tf_op jit(solution)/shard_map/ppermute | solution.py:20
  33.5 8.6 %collective-permute-start.4 = (bf16[128,1024]{1,0:T(8,128)(2,1)S(1)}, bf16[128,1024]{1,0:T(8,128)(2,1)S(1)}, u32[]{:S(2)}, u32[]{:S(2)}) collective-permute-start(bf16[128,1024]{1,0:T(8,128)(2,1)S(1)} %collective-permute-done.2), channel_id=1, source_target_pairs={{0,1},{1,2},{2,3},{3,4},{4,5},{5,6},{6,7},{7,8},{8,9},{9,10},{10,1... | collective-permute-start | bytes 786440 | tf_op jit(solution)/shard_map/ppermute | solution.py:17
  33.5 9.7 %collective-permute-start.5 = (bf16[128,1024]{1,0:T(8,128)(2,1)S(1)}, bf16[128,1024]{1,0:T(8,128)(2,1)S(1)}, u32[]{:S(2)}, u32[]{:S(2)}) collective-permute-start(bf16[128,1024]{1,0:T(8,128)(2,1)S(1)} %collective-permute-done.3), channel_id=1, source_target_pairs={{0,15},{1,0},{2,1},{3,2},{4,3},{5,4},{6,5},{7,6},{8,7},{9,8},{10,9... | collective-permute-start | bytes 786440 | tf_op jit(solution)/shard_map/ppermute | solution.py:20
  42.1 8.6 %collective-permute-start.6 = (bf16[128,1024]{1,0:T(8,128)(2,1)S(1)}, bf16[128,1024]{1,0:T(8,128)(2,1)S(1)}, u32[]{:S(2)}, u32[]{:S(2)}) collective-permute-start(bf16[128,1024]{1,0:T(8,128)(2,1)S(1)} %collective-permute-done.4), channel_id=1, source_target_pairs={{0,1},{1,2},{2,3},{3,4},{4,5},{5,6},{6,7},{7,8},{8,9},{9,10},{10,1... | collective-permute-start | bytes 786440 | tf_op jit(solution)/shard_map/ppermute | solution.py:17
  43.2 9.0 %collective-permute-start.7 = (bf16[128,1024]{1,0:T(8,128)(2,1)S(1)}, bf16[128,1024]{1,0:T(8,128)(2,1)S(1)}, u32[]{:S(2)}, u32[]{:S(2)}) collective-permute-start(bf16[128,1024]{1,0:T(8,128)(2,1)S(1)} %collective-permute-done.5), channel_id=1, source_target_pairs={{0,15},{1,0},{2,1},{3,2},{4,3},{5,4},{6,5},{7,6},{8,7},{9,8},{10,9... | collective-permute-start | bytes 786440 | tf_op jit(solution)/shard_map/ppermute | solution.py:20
  50.7 8.6 %collective-permute-start.8 = (bf16[128,1024]{1,0:T(8,128)(2,1)S(1)}, bf16[128,1024]{1,0:T(8,128)(2,1)S(1)}, u32[]{:S(2)}, u32[]{:S(2)}) collective-permute-start(bf16[128,1024]{1,0:T(8,128)(2,1)S(1)} %collective-permute-done.6), channel_id=1, source_target_pairs={{0,1},{1,2},{2,3},{3,4},{4,5},{5,6},{6,7},{7,8},{8,9},{9,10},{10,1... | collective-permute-start | bytes 786440 | tf_op jit(solution)/shard_map/ppermute | solution.py:17
  52.1 8.6 %collective-permute-start.9 = (bf16[128,1024]{1,0:T(8,128)(2,1)S(1)}, bf16[128,1024]{1,0:T(8,128)(2,1)S(1)}, u32[]{:S(2)}, u32[]{:S(2)}) collective-permute-start(bf16[128,1024]{1,0:T(8,128)(2,1)S(1)} %collective-permute-done.7), channel_id=1, source_target_pairs={{0,15},{1,0},{2,1},{3,2},{4,3},{5,4},{6,5},{7,6},{8,7},{9,8},{10,9... | collective-permute-start | bytes 786440 | tf_op jit(solution)/shard_map/ppermute | solution.py:20
  59.3 8.6 %collective-permute-start.10 = (bf16[128,1024]{1,0:T(8,128)(2,1)S(1)}, bf16[128,1024]{1,0:T(8,128)(2,1)S(1)}, u32[]{:S(2)}, u32[]{:S(2)}) collective-permute-start(bf16[128,1024]{1,0:T(8,128)(2,1)S(1)} %collective-permute-done.8), channel_id=1, source_target_pairs={{0,1},{1,2},{2,3},{3,4},{4,5},{5,6},{6,7},{7,8},{8,9},{9,10},{10,1... | collective-permute-start | bytes 786440 | tf_op jit(solution)/shard_map/ppermute | solution.py:17
  60.8 8.6 %collective-permute-start.11 = (bf16[128,1024]{1,0:T(8,128)(2,1)S(1)}, bf16[128,1024]{1,0:T(8,128)(2,1)S(1)}, u32[]{:S(2)}, u32[]{:S(2)}) collective-permute-start(bf16[128,1024]{1,0:T(8,128)(2,1)S(1)} %collective-permute-done.9), channel_id=1, source_target_pairs={{0,15},{1,0},{2,1},{3,2},{4,3},{5,4},{6,5},{7,6},{8,7},{9,8},{10,9... | collective-permute-start | bytes 786440 | tf_op jit(solution)/shard_map/ppermute | solution.py:20
  67.9 8.6 %collective-permute-start.12 = (bf16[128,1024]{1,0:T(8,128)(2,1)S(1)}, bf16[128,1024]{1,0:T(8,128)(2,1)S(1)}, u32[]{:S(2)}, u32[]{:S(2)}) collective-permute-start(bf16[128,1024]{1,0:T(8,128)(2,1)S(1)} %collective-permute-done.10), channel_id=1, source_target_pairs={{0,1},{1,2},{2,3},{3,4},{4,5},{5,6},{6,7},{7,8},{8,9},{9,10},{10,1... | collective-permute-start | bytes 786440 | tf_op jit(solution)/shard_map/ppermute | solution.py:17
  69.3 8.6 %collective-permute-start.13 = (bf16[128,1024]{1,0:T(8,128)(2,1)S(1)}, bf16[128,1024]{1,0:T(8,128)(2,1)S(1)}, u32[]{:S(2)}, u32[]{:S(2)}) collective-permute-start(bf16[128,1024]{1,0:T(8,128)(2,1)S(1)} %collective-permute-done.11), channel_id=1, source_target_pairs={{0,15},{1,0},{2,1},{3,2},{4,3},{5,4},{6,5},{7,6},{8,7},{9,8},{10,9... | collective-permute-start | bytes 786440 | tf_op jit(solution)/shard_map/ppermute | solution.py:20
  76.5 8.5 %collective-permute-start.14 = (bf16[128,1024]{1,0:T(8,128)(2,1)S(1)}, bf16[128,1024]{1,0:T(8,128)(2,1)S(1)}, u32[]{:S(2)}, u32[]{:S(2)}) collective-permute-start(bf16[128,1024]{1,0:T(8,128)(2,1)S(1)} %collective-permute-done.12), channel_id=1, source_target_pairs={{0,1},{1,2},{2,3},{3,4},{4,5},{5,6},{6,7},{7,8},{8,9},{9,10},{10,1... | collective-permute-start | bytes 786440 | tf_op jit(solution)/shard_map/ppermute | solution.py:17
  102.0 2.0 copy-start
